TPU v7x, 512 devices: a whole 4x4x16 slice. The times are simulated.
512 devices in a mesh: gx: 32 (over z, y_lo), gy: 16 (over y_hi, x, core).
Axes of the slice: x: 4, y: 4 (y_hi: 2, y_lo: 2; y = y_hi * 2 + y_lo), z: 16, core: 2. Of those that a mesh axis runs over, the one named last changes fastest.
Arguments:
- spectrum: float32 [32, 32, 32, 32], P('gx', 'gy'), may hold values from -6 to 6
- spec_weights: float32 [4, 32, 32, 32, 32], P(None, 'gx', 'gy'), may hold values from -1 to 1
- pointwise: bfloat16 [4, 512, 256, 128], P(None, 'gx', 'gy'), may hold values from -6 to 6
- mode_counts: int32 [3], replicated, may hold values from 8 to 16, as said below
- flags: int32 [512, 256], P('gx', 'gy'), may hold values from 0 to 2
Outputs:
- field_grad: bfloat16 [4, 512, 256, 128], P(None, 'gx', 'gy')
- grad_weights: float32 [4, 32, 32, 32, 32], P(None, 'gx', 'gy')
Inputs may be any that keep to these rules, and one draw needn't show every extreme that they name: `mode_counts`: entry a is the number of retained frequencies along x, y, z in turn; one entry equals 16. `flags`: 0 marks a fluid column, 1 a solid wall column, 2 an inflow column.
All inputs are finite; a program needn't handle non-finite values.
Results may differ from a plain program's by a relative error of at most 0.001.
Values sent between devices are 32-bit elements; how exact they have to be, the bound alone decides.
No kernel may reach another device: no remote copies, remote signals or barrier semaphores. Data moves between devices by JAX's collectives and lax.ppermute only.
A program may use at most 64 MiB of HBM per device.

v0:
```python
import math

import jax
import jax.numpy as jnp
from jax import lax
from jax.sharding import PartitionSpec as P

viscosity = 0.1
penalty = 2.0
inflow_speed = 1.0
highest = lax.Precision.HIGHEST


def padded_2(cells, sides, width):
    for axis, dim in sides:
        count = lax.axis_size(axis)
        head = lax.slice_in_dim(cells, 0, width, axis=dim)
        tail = lax.slice_in_dim(cells, cells.shape[dim] - width, cells.shape[dim], axis=dim)
        cells = jnp.concatenate(
            [
                lax.ppermute(tail, axis, [(i, (i + 1) % count) for i in range(count)]),
                cells,
                lax.ppermute(head, axis, [((i + 1) % count, i) for i in range(count)]),
            ],
            axis=dim,
        )
    return cells


def mode_basis(count, length, start, cells, half_modes):
    indices = jnp.arange(2 * half_modes, dtype=jnp.int32)
    freqs = jnp.where(indices < half_modes, indices, indices - half_modes + 1)
    places = start + jnp.arange(cells, dtype=jnp.int32)
    phases = freqs[:, None] * places[None, :] % length
    angles = phases.astype(jnp.float32) * jnp.float32(2.0 * math.pi / length)
    values = jnp.where(indices[:, None] < half_modes, jnp.cos(angles), jnp.sin(angles))
    keep = indices % half_modes < count
    return jnp.where(keep[:, None], values, jnp.float32(0.0)) * jnp.float32(
        math.sqrt(1.0 / half_modes)
    )


def interior(values):
    return values[..., 1:-1, 1:-1, :]


def diff_x(values):
    return (values[..., 2:, 1:-1, :] - values[..., :-2, 1:-1, :]) * 0.5


def diff_y(values):
    return (values[..., 1:-1, 2:, :] - values[..., 1:-1, :-2, :]) * 0.5


def diff_z(values):
    middle = interior(values)
    return (jnp.roll(middle, -1, -1) - jnp.roll(middle, 1, -1)) * 0.5


def laplace(values):
    middle = interior(values)
    total = values[..., 2:, 1:-1, :] + values[..., :-2, 1:-1, :]
    total = total + values[..., 1:-1, 2:, :] + values[..., 1:-1, :-2, :]
    total = total + jnp.roll(middle, -1, -1) + jnp.roll(middle, 1, -1)
    return total - 6.0 * middle


def wall_term(velocity, flags):
    solid = (flags > 0)[:, :, None]
    inflow = (flags == 2)[:, :, None]
    target = jnp.where(inflow, jnp.float32(inflow_speed), jnp.float32(0.0))
    offsets = jnp.stack([target, jnp.zeros_like(target), jnp.zeros_like(target)])
    return penalty * jnp.where(solid[None], velocity - offsets, jnp.float32(0.0))


def residuals(padded):
    velocity = padded[:3]
    pressure = padded[3]
    slope_x = diff_x(velocity)
    slope_y = diff_y(velocity)
    slope_z = diff_z(velocity)
    inside = interior(velocity)
    divergence = slope_x[0] + slope_y[1] + slope_z[2]
    press = jnp.stack([diff_x(pressure), diff_y(pressure), diff_z(pressure)])
    resid = (
        inside[0] * slope_x
        + inside[1] * slope_y
        + inside[2] * slope_z
        + press
        - viscosity * laplace(velocity)
    )
    return (divergence, resid, (slope_x, slope_y, slope_z))


def adjoint(vel_cycle, beside_all, slopes, flags):
    div_cycle = beside_all[0]
    resid_cycle = beside_all[1:]
    resid = interior(resid_cycle)
    velocity = interior(vel_cycle)
    slope_x, slope_y, slope_z = slopes
    back = -jnp.stack([diff_x(div_cycle), diff_y(div_cycle), diff_z(div_cycle)])
    back = back + jnp.stack(
        [jnp.sum(resid * slope_x, 0), jnp.sum(resid * slope_y, 0), jnp.sum(resid * slope_z, 0)]
    )
    back = back - (
        diff_x(vel_cycle[0] * resid_cycle)
        + diff_y(vel_cycle[1] * resid_cycle)
        + diff_z(vel_cycle[2] * resid_cycle)
    )
    back = back - viscosity * laplace(resid_cycle)
    back = back + wall_term(velocity, flags)
    back_pressure = -(diff_x(resid_cycle[0]) + diff_y(resid_cycle[1]) + diff_z(resid_cycle[2]))
    return jnp.concatenate([back, back_pressure[None]], 0)


def body(spectrum, spec_weights, pointwise, mode_counts, flags):
    half_modes = spectrum.shape[3] // 2
    mode_span = 2 * half_modes
    local_freqs = spectrum.shape[1]
    cells_x = pointwise.shape[1]
    cells_y = pointwise.shape[2]
    cells_z = pointwise.shape[3]
    across_x = lax.axis_size("gx")
    across_y = lax.axis_size("gy")
    total_x = cells_x * across_x
    total_y = cells_y * across_y
    basis_x = mode_basis(
        mode_counts[0], total_x, lax.axis_index("gx") * cells_x, cells_x, half_modes
    )
    basis_y = mode_basis(
        mode_counts[1], total_y, lax.axis_index("gy") * cells_y, cells_y, half_modes
    )
    basis_z = mode_basis(mode_counts[2], cells_z, 0, cells_z, half_modes)
    partial_value = jnp.einsum("ocprq,cprq->oprq", spec_weights, spectrum, precision=highest)
    summed = lax.psum(partial_value, "gx")
    spectrum_all = lax.all_gather(summed, "gy", axis=1, tiled=True)
    section = jnp.einsum("oprq,px->oxrq", spectrum_all, basis_x, precision=highest)
    section = jnp.einsum("oxrq,ry->oxyq", section, basis_y, precision=highest)
    fields = jnp.einsum("oxyq,qz->oxyz", section, basis_z, precision=highest) + pointwise.astype(
        jnp.float32
    )
    padded = padded_2(fields, (("gx", 1), ("gy", 2)), 1)
    divergence, resid, slopes = residuals(padded)
    stacked = jnp.concatenate([divergence[None], resid], 0)
    beside_all = padded_2(stacked, (("gx", 1), ("gy", 2)), 1)
    vel_cycle = padded[:3]
    grad_field = adjoint(vel_cycle, beside_all, slopes, flags)
    section = jnp.einsum("oxyz,qz->oxyq", grad_field, basis_z, precision=highest)
    section = jnp.einsum("oxyq,ry->oxrq", section, basis_y, precision=highest)
    projected = jnp.einsum("oxrq,px->oprq", section, basis_x, precision=highest)
    total = lax.psum(projected, ("gx", "gy"))
    mixed_grad = lax.dynamic_slice_in_dim(total, lax.axis_index("gy") * local_freqs, local_freqs, 1)
    scale = mode_span**1.5 / math.sqrt(total_x * total_y * cells_z)
    grad_weights = jnp.float32(scale) * mixed_grad[:, None] * spectrum[None]
    return (grad_field.astype(jnp.bfloat16), grad_weights)


def solution(mesh):
    return jax.shard_map(
        body,
        mesh=mesh,
        in_specs=(
            P("gx", "gy", None, None),
            P(None, "gx", "gy", None, None),
            P(None, "gx", "gy", None),
            P(),
            P("gx", "gy"),
        ),
        out_specs=(P(None, "gx", "gy", None), P(None, "gx", "gy", None, None)),
        check_vma=False,
    )
```

profile of v0, /device:TPU:1, one launch (start us, length us, event | category | flops | bytes accessed | tf_op | source)
XLA Modules:
  0.0 715.0 jit_solution(7231251280529691835)
XLA Ops:
  7.2 0.9 bitcast_multiply_fusion
  8.2 102.1 %psum.14 = f32[4,2,32,32]{3,2,1,0:T(8,128)S(1)} all-reduce(f32[4,2,32,32]{3,2,1,0:T(8,128)S(1)} %bitcast_multiply_fusion), channel_id=1, replica_groups=mesh['gx'=32,'gy'=16] {'gx'}, use_global_device_ids=true, to_apply=%region_0.1 | all-reduce | flops 8192 | bytes 65536 | tf_op jit(solution)/shard_map/psum | solution.py:135
  110.2 58.0 %all_gather.3 = f32[4,32,32,32]{3,2,1,0:T(8,128)S(1)} all-gather(f32[4,2,32,32]{3,2,1,0:T(8,128)S(1)} %psum.14), channel_id=1, replica_groups=mesh['gx'=32,'gy'=16] {'gy'}, dimensions={1}, use_global_device_ids=true | all-gather | bytes 557056 | tf_op jit(solution)/shard_map/all_gather | solution.py:136
  168.2 0.7 fusion.112
  168.9 0.7 iota_compare_fusion
  169.6 0.7 broadcast_compare_fusion.3
  170.2 0.7 broadcast_compare_fusion.1
  170.9 2.3 fusion.2
  173.2 1.0 convolution_bitcast_fusion.1
  174.2 0.7 convolution_add_fusion
  175.0 1.9 collective-permute-start.1
  176.9 5.5 collective-permute-start
  182.6 0.2 fusion.106
  182.8 0.6 collective-permute-done
  183.4 1.9 collective-permute-start.3
  185.4 3.2 collective-permute-start.2
  188.6 2.0 collective-permute-done.2
  191.3 0.6 multiply_reduce_fusion.2
  191.9 5.8 collective-permute-start.5
  197.7 1.9 collective-permute-start.4
  199.8 4.7 collective-permute-done.4
  204.5 8.5 %collective-permute-start.7 = (f32[4,18,1,128]{3,2,1,0:T(1,128)S(1)}, f32[4,18,1,128]{3,2,1,0:T(1,128)S(1)}, u32[]{:S(2)}, u32[]{:S(2)}) collective-permute-start(f32[4,18,1,128]{3,2,1,0:T(1,128)S(1)} %get-tuple-element.29), channel_id=1, source_target_pairs={{1,0},{2,1},{3,2},{4,3},{5,4},{6,5},{7,6},{8,7},{9,8},{10,9},{11,1... | collective-permute-start | bytes 110600 | tf_op jit(solution)/shard_map/ppermute | solution.py:23
  213.0 2.1 collective-permute-start.6
  215.3 4.9 collective-permute-done.6
  221.7 0.9 fusion.16
  222.6 0.7 fusion.8
  223.3 1.1 fusion.59
  224.5 3.6 convolution_bitcast_fusion
  228.2 0.7 fusion.9
  228.9 477.4 %all-reduce.3.cloned.1.call-done = f32[4,32,32,32]{3,1,2,0:T(8,128)} async-done(((f32[4,32,32,32]{3,1,2,0:T(8,128)}), f32[4,32,32,32]{3,1,2,0:T(8,128)}) %all-reduce.3.cloned.1.call-update) | async-done | bytes 524304 | tf_op jit(solution)/shard_map/psum | solution.py:151
  706.3 1.1 multiply_bitcast_fusion
  707.4 0.7 copy.18
  (49 shorter events, 2.9 us)
Async XLA Ops:
  7.2 161.0 %copy-start.3 = (s32[3]{0:T(128)S(1)}, s32[3]{0:T(128)}, u32[]{:S(2)}) copy-start(s32[3]{0:T(128)} %param.8) | copy-start | bytes 40
  7.2 699.2 %all-reduce.3.cloned.1.call-start = ((), (), s32[]{:S(2)}) async-start(), calls=%async_computation | async-start | bytes 4194304 | tf_op jit(solution)/shard_map/psum | solution.py:151
  170.9 3.3 copy-start
  175.0 7.8 %copy-start.2 = (s32[16,16]{1,0:T(8,128)S(1)}, s32[16,16]{1,0:T(8,128)}, u32[]{:S(2)}) copy-start(s32[16,16]{1,0:T(8,128)} %param.9) | copy-start | bytes 3076
  175.0 7.8 %collective-permute-start.1 = (f32[4,1,16,128]{3,2,1,0:T(8,128)S(1)}, f32[4,1,16,128]{3,2,1,0:T(8,128)S(1)}, u32[]{:S(2)}, u32[]{:S(2)}) collective-permute-start(f32[4,1,16,128]{3,2,1,0:T(8,128)S(1)} %get-tuple-element.42), channel_id=1, source_target_pairs={{0,16},{16,32},{32,48},{48,64},{64,80},{80,96},{96,112},{112,128},... | collective-permute-start | bytes 98312 | tf_op jit(solution)/shard_map/ppermute | solution.py:21
  176.9 6.5 collective-permute-start
  183.4 5.2 collective-permute-start.3
  185.4 5.3 collective-permute-start.2
  191.9 7.9 %collective-permute-start.5 = (f32[4,1,16,128]{3,2,1,0:T(8,128)S(1)}, f32[4,1,16,128]{3,2,1,0:T(8,128)S(1)}, u32[]{:S(2)}, u32[]{:S(2)}) collective-permute-start(f32[4,1,16,128]{3,2,1,0:T(8,128)S(1)} %get-tuple-element.33), channel_id=1, source_target_pairs={{16,0},{32,16},{48,32},{64,48},{80,64},{96,80},{112,96},{128,112},... | collective-permute-start | bytes 98312 | tf_op jit(solution)/shard_map/ppermute | solution.py:23
  197.7 6.8 collective-permute-start.4
  204.5 10.8 %collective-permute-start.7 = (f32[4,18,1,128]{3,2,1,0:T(1,128)S(1)}, f32[4,18,1,128]{3,2,1,0:T(1,128)S(1)}, u32[]{:S(2)}, u32[]{:S(2)}) collective-permute-start(f32[4,18,1,128]{3,2,1,0:T(1,128)S(1)} %get-tuple-element.29), channel_id=1, source_target_pairs={{1,0},{2,1},{3,2},{4,3},{5,4},{6,5},{7,6},{8,7},{9,8},{10,9},{11,1... | collective-permute-start | bytes 110600 | tf_op jit(solution)/shard_map/ppermute | solution.py:23
  213.0 7.2 %collective-permute-start.6 = (f32[4,18,1,128]{3,2,1,0:T(1,128)S(1)}, f32[4,18,1,128]{3,2,1,0:T(1,128)S(1)}, u32[]{:S(2)}, u32[]{:S(2)}) collective-permute-start(f32[4,18,1,128]{3,2,1,0:T(1,128)S(1)} %get-tuple-element.28), channel_id=1, source_target_pairs={{0,1},{1,2},{2,3},{3,4},{4,5},{5,6},{6,7},{7,8},{8,9},{9,10},{10,1... | collective-permute-start | bytes 110600 | tf_op jit(solution)/shard_map/ppermute | solution.py:21
  224.5 3.6 copy-start.1
Sparse Core Ops, SparseCore 0:
  228.2 478.0 all-reduce.2
where the time goes:
time: 715 us
  waiting for transfers between devices  490 us (69%)
  blocking collectives  160 us (22%)
  starting transfers between devices  30.8 us (4%)
  between operations  14.4 us (2%)
  matrix products  9.45 us (1%)
  other arithmetic  7.35 us (1%)
    psum x1, waiting for transfers between devices, body(): total = lax.psum(projected, ('gx', 'gy'))  477 us
    psum x1, blocking collectives, body(): summed = lax.psum(partial_value, 'gx')  102 us
    all_gather x1, blocking collectives, body(): spectrum_all = lax.all_gather(summed, 'gy', axis=1, tiled=True)  58 us
    ppermute x4, starting transfers between devices, padded_2(): lax.ppermute(head, axis, [((i + 1) % count, i) for i in range(count)])  22.9 us
  transfers between devices with their start and end apart: 9, of which 5 were waited for; matrix products, arithmetic and copies ran while one was open for 0% of the time, Pallas kernels for 0%

commit v1 on v0

--- a/solution.py
+++ b/solution.py
@@ -8,23 +8,7 @@
 viscosity = 0.1
 penalty = 2.0
 inflow_speed = 1.0
-highest = lax.Precision.HIGHEST
-
-
-def padded_2(cells, sides, width):
-    for axis, dim in sides:
-        count = lax.axis_size(axis)
-        head = lax.slice_in_dim(cells, 0, width, axis=dim)
-        tail = lax.slice_in_dim(cells, cells.shape[dim] - width, cells.shape[dim], axis=dim)
-        cells = jnp.concatenate(
-            [
-                lax.ppermute(tail, axis, [(i, (i + 1) % count) for i in range(count)]),
-                cells,
-                lax.ppermute(head, axis, [((i + 1) % count, i) for i in range(count)]),
-            ],
-            axis=dim,
-        )
-    return cells
+high = lax.Precision.HIGH
 
 
 def mode_basis(count, length, start, cells, half_modes):
@@ -113,10 +97,39 @@
     return jnp.concatenate([back, back_pressure[None]], 0)
 
 
+def shift_pair(head, tail, axis):
+    count = lax.axis_size(axis)
+    before = lax.ppermute(tail, axis, [(i, (i + 1) % count) for i in range(count)])
+    after = lax.ppermute(head, axis, [((i + 1) % count, i) for i in range(count)])
+    return before, after
+
+
+def extended(cells, axis, dim, width):
+    size = cells.shape[dim]
+    head = lax.slice_in_dim(cells, 0, width, axis=dim).astype(jnp.float32)
+    tail = lax.slice_in_dim(cells, size - width, size, axis=dim).astype(jnp.float32)
+    before, after = shift_pair(head, tail, axis)
+    return jnp.concatenate([before, cells.astype(jnp.float32), after], axis=dim)
+
+
+def exchange(chunks, axis):
+    return lax.all_to_all(chunks, axis, 0, 0, tiled=True)
+
+
+def reduce_scattered(chunks, axis):
+    return jnp.sum(exchange(chunks, axis), 0)
+
+
+def gathered(part, axis):
+    count = lax.axis_size(axis)
+    return exchange(jnp.broadcast_to(part[None], (count,) + part.shape), axis)
+
+
 def body(spectrum, spec_weights, pointwise, mode_counts, flags):
     half_modes = spectrum.shape[3] // 2
     mode_span = 2 * half_modes
     local_freqs = spectrum.shape[1]
+    parts = pointwise.shape[0]
     cells_x = pointwise.shape[1]
     cells_y = pointwise.shape[2]
     cells_z = pointwise.shape[3]
@@ -124,32 +137,32 @@
     across_y = lax.axis_size("gy")
     total_x = cells_x * across_x
     total_y = cells_y * across_y
-    basis_x = mode_basis(
-        mode_counts[0], total_x, lax.axis_index("gx") * cells_x, cells_x, half_modes
-    )
-    basis_y = mode_basis(
-        mode_counts[1], total_y, lax.axis_index("gy") * cells_y, cells_y, half_modes
-    )
+    first_x = lax.axis_index("gx") * cells_x
+    first_y = lax.axis_index("gy") * cells_y
+    basis_x = mode_basis(mode_counts[0], total_x, first_x - 2, cells_x + 4, half_modes)
+    basis_y = mode_basis(mode_counts[1], total_y, first_y - 2, cells_y + 4, half_modes)
     basis_z = mode_basis(mode_counts[2], cells_z, 0, cells_z, half_modes)
-    partial_value = jnp.einsum("ocprq,cprq->oprq", spec_weights, spectrum, precision=highest)
-    summed = lax.psum(partial_value, "gx")
-    spectrum_all = lax.all_gather(summed, "gy", axis=1, tiled=True)
-    section = jnp.einsum("oprq,px->oxrq", spectrum_all, basis_x, precision=highest)
-    section = jnp.einsum("oxrq,ry->oxyq", section, basis_y, precision=highest)
-    fields = jnp.einsum("oxyq,qz->oxyz", section, basis_z, precision=highest) + pointwise.astype(
-        jnp.float32
-    )
-    padded = padded_2(fields, (("gx", 1), ("gy", 2)), 1)
-    divergence, resid, slopes = residuals(padded)
+    wide = extended(pointwise, "gx", 1, 2)
+    wide = extended(wide, "gy", 2, 2)
+    partial_value = jnp.sum(spec_weights * spectrum[None], 1)
+    chunks = jnp.transpose(partial_value, (1, 0, 2, 3)).reshape(across_x, -1)
+    modes = gathered(reduce_scattered(chunks, "gx"), "gx")
+    modes = gathered(modes.reshape(-1), "gy").reshape(mode_span, parts, mode_span, mode_span)
+    section = jnp.einsum("porq,px->oxrq", modes, basis_x, precision=high)
+    section = jnp.einsum("oxrq,ry->oxyq", section, basis_y, precision=high)
+    fields = jnp.einsum("oxyq,qz->oxyz", section, basis_z, precision=high) + wide
+    divergence, resid, slopes = residuals(fields)
     stacked = jnp.concatenate([divergence[None], resid], 0)
-    beside_all = padded_2(stacked, (("gx", 1), ("gy", 2)), 1)
-    vel_cycle = padded[:3]
-    grad_field = adjoint(vel_cycle, beside_all, slopes, flags)
-    section = jnp.einsum("oxyz,qz->oxyq", grad_field, basis_z, precision=highest)
-    section = jnp.einsum("oxyq,ry->oxrq", section, basis_y, precision=highest)
-    projected = jnp.einsum("oxrq,px->oprq", section, basis_x, precision=highest)
-    total = lax.psum(projected, ("gx", "gy"))
-    mixed_grad = lax.dynamic_slice_in_dim(total, lax.axis_index("gy") * local_freqs, local_freqs, 1)
+    vel_cycle = fields[:3, 1:-1, 1:-1]
+    inner = tuple(interior(slope) for slope in slopes)
+    grad_field = adjoint(vel_cycle, stacked, inner, flags)
+    section = jnp.einsum("oxyz,qz->oxyq", grad_field, basis_z, precision=high)
+    section = jnp.einsum("oxyq,ry->oxrq", section, basis_y[:, 2:-2], precision=high)
+    projected = jnp.einsum("oxrq,px->porq", section, basis_x[:, 2:-2], precision=high)
+    summed = reduce_scattered(projected.reshape(across_y, -1), "gy")
+    summed = reduce_scattered(summed.reshape(across_x, -1), "gx")
+    total = gathered(summed, "gx").reshape(local_freqs, parts, mode_span, mode_span)
+    mixed_grad = jnp.transpose(total, (1, 0, 2, 3))
     scale = mode_span**1.5 / math.sqrt(total_x * total_y * cells_z)
     grad_weights = jnp.float32(scale) * mixed_grad[:, None] * spectrum[None]
     return (grad_field.astype(jnp.bfloat16), grad_weights)

time: 715 us -> 149 us (0.21)
  waiting for transfers between devices: 490 us -> 33.7 us
  blocking collectives: 160 us -> 33.8 us
  starting transfers between devices: 30.8 us -> 47.1 us
  between operations: 14.4 us -> 1.17 us
  local copies, waits for them, and re-layouts: 3.18 us -> 10.5 us
    psum x1 -> x0, waiting for transfers between devices: 477 us -> none  [body(): total = lax.psum(projected, ('gx', 'gy'))]
    psum x1 -> x0, blocking collectives: 102 us -> none  [body(): summed = lax.psum(partial_value, 'gx')]
    all_gather x1 -> x0, blocking collectives: 58 us -> none  [body(): spectrum_all = lax.all_gather(summed, 'gy', axis=1, tiled=True)]
    all_to_all x0 -> x2, blocking collectives: none -> 33.8 us  [exchange(): return lax.all_to_all(chunks, axis, 0, 0, tiled=True)]
    all_to_all x0 -> x4, waiting for transfers between devices: none -> 33.7 us  [exchange(): return lax.all_to_all(chunks, axis, 0, 0, tiled=True)]
    all_to_all x0 -> x4, starting transfers between devices: none -> 26.5 us  [exchange(): return lax.all_to_all(chunks, axis, 0, 0, tiled=True)]
    ppermute x8 -> x4, waiting for transfers between devices: 12.2 us -> 0.01 us  [the longest x2 0.01 us: shift_pair(): lax.ppermute(head, axis, [((i + 1) % count, i) for i in range(count)])]
    ppermute x8 -> x4, starting transfers between devices: 30.8 us -> 20.6 us  [the longest x2 15 us: shift_pair(): lax.ppermute(head, axis, [((i + 1) % count, i) for i in range(count)])]
  transfers between devices with their start and end apart: 9 -> 8, of which waited for: 5 -> 4; matrix products, arithmetic and copies ran while one was open for 0% -> 11% of each run, Pallas kernels for 0% -> 0%
where the time goes in v1:
time: 149 us; the launch traced here: 147 us
  starting transfers between devices  47.1 us (32%)
  blocking collectives  33.8 us (23%)
  waiting for transfers between devices  33.7 us (23%)
  other arithmetic  13.6 us (9%)
  local copies, waits for them, and re-layouts  10.5 us (7%)
  matrix products  6.77 us (5%)
    all_to_all x2, blocking collectives, exchange(): return lax.all_to_all(chunks, axis, 0, 0, tiled=True)  33.8 us
    all_to_all x4, waiting for transfers between devices, exchange(): return lax.all_to_all(chunks, axis, 0, 0, tiled=True)  33.7 us
    all_to_all x4, starting transfers between devices, exchange(): return lax.all_to_all(chunks, axis, 0, 0, tiled=True)  26.5 us
    ppermute x2, starting transfers between devices, shift_pair(): lax.ppermute(head, axis, [((i + 1) % count, i) for i in range(count)])  15 us
    ppermute x2, starting transfers between devices, shift_pair(): lax.ppermute(tail, axis, [(i, (i + 1) % count) for i in range(count)])  5.65 us
  transfers between devices with their start and end apart: 8, of which 4 were waited for; matrix products, arithmetic and copies ran while one was open for 11% of the time, Pallas kernels for 0%

profile of v1, /device:TPU:1, one launch (start us, length us, event | category | flops | bytes accessed | tf_op | source)
XLA Modules:
  0.0 146.6 jit_solution(5545712975344122630)
XLA Ops:
  0.6 0.8 slice_convert_fusion.1
  1.5 13.0 %collective-permute-start.1 = (f32[4,2,16,128]{3,2,1,0:T(8,128)S(1)}, f32[4,2,16,128]{3,2,1,0:T(8,128)S(1)}, u32[]{:S(2)}, u32[]{:S(2)}) collective-permute-start(f32[4,2,16,128]{3,2,1,0:T(8,128)S(1)} %get-tuple-element.47), channel_id=1, source_target_pairs={{16,0},{32,16},{48,32},{64,48},{80,64},{96,80},{112,96},{128,112},... | collective-permute-start | bytes 196616 | tf_op jit(solution)/shard_map/ppermute | solution.py:103
  14.4 1.9 %collective-permute-start = (f32[4,2,16,128]{3,2,1,0:T(8,128)S(1)}, f32[4,2,16,128]{3,2,1,0:T(8,128)S(1)}, u32[]{:S(2)}, u32[]{:S(2)}) collective-permute-start(f32[4,2,16,128]{3,2,1,0:T(8,128)S(1)} %get-tuple-element.46), channel_id=1, source_target_pairs={{0,16},{16,32},{32,48},{48,64},{64,80},{80,96},{96,112},{112,128},... | collective-permute-start | bytes 196616 | tf_op jit(solution)/shard_map/ppermute | solution.py:102
  16.4 0.9 multiply_bitcast_fusion.1
  17.3 0.7 all_to_all.39
  18.0 8.3 %all-to-all-start = ((f32[32,1,256]{2,1,0:T(1,128)}), f32[32,1,256]{2,1,0:T(1,128)S(1)}, u32[]{:S(2)}, u32[]{:S(2)}) async-start(f32[32,1,256]{2,1,0:T(1,128)} %all_to_all.39), calls=%async_computation | async-start | bytes 65536 | tf_op jit(solution)/shard_map/all_to_all | solution.py:116
  27.1 1.3 broadcast_compare_fusion
  28.4 1.4 fusion.98
  30.5 8.2 %all-to-all-done = f32[32,1,256]{2,1,0:T(1,128)S(1)} async-done(((f32[32,1,256]{2,1,0:T(1,128)}), f32[32,1,256]{2,1,0:T(1,128)S(1)}, u32[]{:S(2)}, u32[]{:S(2)}) %all-to-all-start) | async-done | bytes 32800 | tf_op jit(solution)/shard_map/all_to_all | solution.py:116
  39.3 4.4 %all-to-all-start.1 = ((f32[32,1,256]{2,1,0:T(1,128)}), f32[32,1,256]{2,1,0:T(1,128)S(1)}, u32[]{:S(2)}, u32[]{:S(2)}) async-start(f32[32,1,256]{2,1,0:T(1,128)} %broadcast_in_dim.113), calls=%async_computation.1 | async-start | bytes 65536 | tf_op jit(solution)/shard_map/all_to_all | solution.py:116
  44.3 11.6 %all-to-all-done.1 = f32[32,1,256]{2,1,0:T(1,128)S(1)} async-done(((f32[32,1,256]{2,1,0:T(1,128)}), f32[32,1,256]{2,1,0:T(1,128)S(1)}, u32[]{:S(2)}, u32[]{:S(2)}) %all-to-all-start.1) | async-done | bytes 32800 | tf_op jit(solution)/shard_map/all_to_all | solution.py:116
  56.0 1.2 broadcast_in_dim.115
  57.2 9.9 %all-to-all-start.2 = ((f32[16,1,8192]{2,1,0:T(1,128)}), f32[16,1,8192]{2,1,0:T(1,128)S(1)}, u32[]{:S(2)}, u32[]{:S(2)}) async-start(f32[16,1,8192]{2,1,0:T(1,128)} %broadcast_in_dim.115), calls=%async_computation.2 | async-start | bytes 1048576 | tf_op jit(solution)/shard_map/all_to_all | solution.py:116
  67.2 0.8 select_multiply_fusion.1
  67.9 1.2 broadcast_compare_fusion.1
  69.9 2.0 %collective-permute-start.3 = (f32[4,20,2,128]{3,2,1,0:T(2,128)}, f32[4,20,2,128]{3,2,1,0:T(2,128)S(1)}, u32[]{:S(2)}, u32[]{:S(2)}) collective-permute-start(f32[4,20,2,128]{3,2,1,0:T(2,128)} %get-tuple-element.45), channel_id=1, source_target_pairs={{1,0},{2,1},{3,2},{4,3},{5,4},{6,5},{7,6},{8,7},{9,8},{10,9},{11,1... | collective-permute-start | bytes 245768 | tf_op jit(solution)/shard_map/ppermute | solution.py:103
  71.9 3.7 %collective-permute-start.2 = (f32[4,20,2,128]{3,2,1,0:T(2,128)S(1)}, f32[4,20,2,128]{3,2,1,0:T(2,128)S(1)}, u32[]{:S(2)}, u32[]{:S(2)}) collective-permute-start(f32[4,20,2,128]{3,2,1,0:T(2,128)S(1)} %get-tuple-element.44), channel_id=1, source_target_pairs={{0,1},{1,2},{2,3},{3,4},{4,5},{5,6},{6,7},{7,8},{8,9},{9,10},{10,1... | collective-permute-start | bytes 245768 | tf_op jit(solution)/shard_map/ppermute | solution.py:102
  75.6 2.4 %all-to-all-done.2 = f32[16,1,8192]{2,1,0:T(1,128)S(1)} async-done(((f32[16,1,8192]{2,1,0:T(1,128)}), f32[16,1,8192]{2,1,0:T(1,128)S(1)}, u32[]{:S(2)}, u32[]{:S(2)}) %all-to-all-start.2) | async-done | bytes 524320 | tf_op jit(solution)/shard_map/all_to_all | solution.py:116
  78.1 1.2 reduce.3
  80.0 2.6 %fusion.2 = f32[4,20,32,32]{3,1,2,0:T(8,128)S(1)} fusion(f32[32,4,32,32]{3,2,1,0:T(8,128)S(1)} %reshape.207, s32[20]{0:T(128)} %copy-done.5, s32[32]{0:T(128)S(1)} %add_select_fusion.3, pred[32]{0:T(512)(128)(4,1)} %copy-done.6, pred[32]{0:T(512)(128)(4,1)S(1)} %get-tuple-element.69), kind=kOutput, calls=%fused_computation.2 | convolution fusion | flops 15739520 | bytes 852240 | tf_op jit(solution)/shard_map/porq,px->oxrq/dot_general | solution.py:151
  82.7 0.7 convolution_bitcast_fusion.1
  83.5 0.7 maximum_add_fusion
  85.4 0.8 broadcast_multiply_fusion
  89.0 0.9 fusion.15
  91.1 1.6 %fusion.6 = f32[32,4,32,32]{3,0,2,1:T(8,128)S(1)} fusion(f32[4,16,32,32]{3,2,1,0:T(8,128)S(1)} %convolution_bitcast_fusion, f32[32,20]{0,1:T(8,128)S(1)} %copy-done.2), kind=kOutput, calls=%fused_computation.6 | convolution fusion | flops 12582912 | bytes 1581056 | tf_op jit(solution)/shard_map/oxrq,px->porq/dot_general | solution.py:161
  92.7 1.2 copy.74
  93.9 0.9 all_to_all.40
  94.9 18.6 %all_to_all.47 = f32[16,1,8192]{2,1,0:T(1,128)S(1)} all-to-all(f32[16,1,8192]{2,1,0:T(1,128)S(1)} %all_to_all.40), channel_id=1, replica_groups=mesh['gx'=32,'gy'=16] {'gy'}, dimensions={0} | all-to-all | bytes 1048576 | tf_op jit(solution)/shard_map/all_to_all | solution.py:116
  113.8 15.2 %all_to_all.48 = f32[32,1,256]{2,1,0:T(1,128)S(1)} all-to-all(f32[32,1,256]{2,1,0:T(1,128)S(1)} %bitcast.116), channel_id=1, replica_groups=mesh['gx'=32,'gy'=16] {'gx'}, dimensions={0} | all-to-all | bytes 65536 | tf_op jit(solution)/shard_map/all_to_all | solution.py:116
  129.7 3.9 %all-to-all-start.5 = ((f32[32,1,256]{2,1,0:T(1,128)}), f32[32,1,256]{2,1,0:T(1,128)S(1)}, u32[]{:S(2)}, u32[]{:S(2)}) async-start(f32[32,1,256]{2,1,0:T(1,128)} %broadcast_in_dim.124), calls=%async_computation.5 | async-start | bytes 65536 | tf_op jit(solution)/shard_map/all_to_all | solution.py:116
  133.6 0.7 fusion.12
  134.3 11.4 %all-to-all-done.5 = f32[32,1,256]{2,1,0:T(1,128)S(1)} async-done(((f32[32,1,256]{2,1,0:T(1,128)}), f32[32,1,256]{2,1,0:T(1,128)S(1)}, u32[]{:S(2)}, u32[]{:S(2)}) %all-to-all-start.5) | async-done | bytes 32800 | tf_op jit(solution)/shard_map/all_to_all | solution.py:116
  (77 shorter events, 11.0 us)
Async XLA Ops:
  0.6 66.5 %copy-start = (bf16[4,16,16,128]{3,2,1,0:T(8,128)(2,1)S(1)}, bf16[4,16,16,128]{3,2,1,0:T(8,128)(2,1)}, u32[]{:S(2)}) copy-start(bf16[4,16,16,128]{3,2,1,0:T(8,128)(2,1)} %param.7) | copy-start | bytes 786436
  1.5 67.7 %collective-permute-start.1 = (f32[4,2,16,128]{3,2,1,0:T(8,128)S(1)}, f32[4,2,16,128]{3,2,1,0:T(8,128)S(1)}, u32[]{:S(2)}, u32[]{:S(2)}) collective-permute-start(f32[4,2,16,128]{3,2,1,0:T(8,128)S(1)} %get-tuple-element.47), channel_id=1, source_target_pairs={{16,0},{32,16},{48,32},{64,48},{80,64},{96,80},{112,96},{128,112},... | collective-permute-start | bytes 196616 | tf_op jit(solution)/shard_map/ppermute | solution.py:103
  14.4 54.7 %collective-permute-start = (f32[4,2,16,128]{3,2,1,0:T(8,128)S(1)}, f32[4,2,16,128]{3,2,1,0:T(8,128)S(1)}, u32[]{:S(2)}, u32[]{:S(2)}) collective-permute-start(f32[4,2,16,128]{3,2,1,0:T(8,128)S(1)} %get-tuple-element.46), channel_id=1, source_target_pairs={{0,16},{16,32},{32,48},{48,64},{64,80},{80,96},{96,112},{112,128},... | collective-permute-start | bytes 196616 | tf_op jit(solution)/shard_map/ppermute | solution.py:102
  18.0 20.6 %all-to-all-start = ((f32[32,1,256]{2,1,0:T(1,128)}), f32[32,1,256]{2,1,0:T(1,128)S(1)}, u32[]{:S(2)}, u32[]{:S(2)}) async-start(f32[32,1,256]{2,1,0:T(1,128)} %all_to_all.39), calls=%async_computation | async-start | bytes 65536 | tf_op jit(solution)/shard_map/all_to_all | solution.py:116
  29.8 40.0 %copy-start.5 = (s32[20]{0:T(128)}, s32[20]{0:T(128)S(1)}, u32[]{:S(2)}) copy-start(s32[20]{0:T(128)S(1)} %iota_add_fusion) | copy-start | bytes 244
  30.5 39.4 %copy-start.8 = (pred[32]{0:T(512)(128)(4,1)}, pred[32]{0:T(512)(128)(4,1)S(1)}, u32[]{:S(2)}) copy-start(pred[32]{0:T(512)(128)(4,1)S(1)} %get-tuple-element.70) | copy-start | bytes 100
  39.3 16.6 %all-to-all-start.1 = ((f32[32,1,256]{2,1,0:T(1,128)}), f32[32,1,256]{2,1,0:T(1,128)S(1)}, u32[]{:S(2)}, u32[]{:S(2)}) async-start(f32[32,1,256]{2,1,0:T(1,128)} %broadcast_in_dim.113), calls=%async_computation.1 | async-start | bytes 65536 | tf_op jit(solution)/shard_map/all_to_all | solution.py:116
  44.3 25.6 %copy-start.6 = (pred[32]{0:T(512)(128)(4,1)}, pred[32]{0:T(512)(128)(4,1)S(1)}, u32[]{:S(2)}) copy-start(pred[32]{0:T(512)(128)(4,1)S(1)} %broadcast_compare_fusion.2) | copy-start | bytes 100
  57.2 20.9 %all-to-all-start.2 = ((f32[16,1,8192]{2,1,0:T(1,128)}), f32[16,1,8192]{2,1,0:T(1,128)S(1)}, u32[]{:S(2)}, u32[]{:S(2)}) async-start(f32[16,1,8192]{2,1,0:T(1,128)} %broadcast_in_dim.115), calls=%async_computation.2 | async-start | bytes 1048576 | tf_op jit(solution)/shard_map/all_to_all | solution.py:116
  67.1 2.8 %copy-start.10 = (s32[20]{0:T(128)}, s32[20]{0:T(128)S(1)}, u32[]{:S(2)}) copy-start(s32[20]{0:T(128)S(1)} %iota_add_fusion.1) | copy-start | bytes 244
  69.9 13.6 %collective-permute-start.3 = (f32[4,20,2,128]{3,2,1,0:T(2,128)}, f32[4,20,2,128]{3,2,1,0:T(2,128)S(1)}, u32[]{:S(2)}, u32[]{:S(2)}) collective-permute-start(f32[4,20,2,128]{3,2,1,0:T(2,128)} %get-tuple-element.45), channel_id=1, source_target_pairs={{1,0},{2,1},{3,2},{4,3},{5,4},{6,5},{7,6},{8,7},{9,8},{10,9},{11,1... | collective-permute-start | bytes 245768 | tf_op jit(solution)/shard_map/ppermute | solution.py:103
  71.9 11.5 %collective-permute-start.2 = (f32[4,20,2,128]{3,2,1,0:T(2,128)S(1)}, f32[4,20,2,128]{3,2,1,0:T(2,128)S(1)}, u32[]{:S(2)}, u32[]{:S(2)}) collective-permute-start(f32[4,20,2,128]{3,2,1,0:T(2,128)S(1)} %get-tuple-element.44), channel_id=1, source_target_pairs={{0,1},{1,2},{2,3},{3,4},{4,5},{5,6},{6,7},{7,8},{8,9},{9,10},{10,1... | collective-permute-start | bytes 245768 | tf_op jit(solution)/shard_map/ppermute | solution.py:102
  80.0 2.7 %copy-start.9 = (pred[32]{0:T(512)(128)(4,1)S(1)}, pred[32]{0:T(512)(128)(4,1)}, u32[]{:S(2)}) copy-start(pred[32]{0:T(512)(128)(4,1)} %copy-done.8) | copy-start | bytes 100
  80.0 2.7 %copy-start.11 = (s32[20]{0:T(128)S(1)}, s32[20]{0:T(128)}, u32[]{:S(2)}) copy-start(s32[20]{0:T(128)} %copy-done.10) | copy-start | bytes 244
  80.0 3.4 %copy-start.7 = (pred[32]{0:T(512)(128)(4,1)S(1)}, pred[32]{0:T(512)(128)(4,1)}, u32[]{:S(2)}) copy-start(pred[32]{0:T(512)(128)(4,1)} %broadcast_compare_fusion.1) | copy-start | bytes 100
  88.4 0.7 copy-start.4
  89.0 1.4 copy-start.3
  89.9 1.2 copy-start.2
  93.9 39.6 %copy-start.1 = (f32[1,2,32,32]{3,2,1,0:T(8,128)S(1)}, f32[1,2,32,32]{3,2,1,0:T(8,128)}, u32[]{:S(2)}) copy-start(f32[1,2,32,32]{3,2,1,0:T(8,128)} %param.5) | copy-start | bytes 24580
  129.7 16.0 %all-to-all-start.5 = ((f32[32,1,256]{2,1,0:T(1,128)}), f32[32,1,256]{2,1,0:T(1,128)S(1)}, u32[]{:S(2)}, u32[]{:S(2)}) async-start(f32[32,1,256]{2,1,0:T(1,128)} %broadcast_in_dim.124), calls=%async_computation.5 | async-start | bytes 65536 | tf_op jit(solution)/shard_map/all_to_all | solution.py:116

commit v2 on v1

v2 whole, which is shorter than its diff:
```python
import functools
import math

import jax
import jax.numpy as jnp
from jax import lax
from jax.experimental import pallas as pl
from jax.experimental.pallas import tpu as pltpu
from jax.sharding import PartitionSpec as P

viscosity = 0.1
penalty = 2.0
inflow_speed = 1.0
halo = 2
rim = 8


def mode_basis(count, length, places, half_modes):
    indices = jnp.arange(2 * half_modes, dtype=jnp.int32)
    freqs = jnp.where(indices < half_modes, indices, indices - half_modes + 1)
    phases = freqs[:, None] * places[None, :] % length
    angles = phases.astype(jnp.float32) * jnp.float32(2.0 * math.pi / length)
    values = jnp.where(indices[:, None] < half_modes, jnp.cos(angles), jnp.sin(angles))
    keep = indices % half_modes < count
    return jnp.where(keep[:, None], values, jnp.float32(0.0)) * jnp.float32(
        math.sqrt(1.0 / half_modes)
    )


def halves(values):
    high = values.astype(jnp.bfloat16)
    low = (values - high.astype(jnp.float32)).astype(jnp.bfloat16)
    return high, low


def stacked_rows(values):
    high, low = halves(values)
    return jnp.concatenate([high, low, high], axis=0)


def stacked_lanes(values, width):
    high, low = halves(values)
    lanes = lax.broadcasted_iota(jnp.int32, values.shape, 1)
    picked = jnp.where(lanes < 2 * width, high.astype(jnp.float32), low.astype(jnp.float32))
    return picked.astype(jnp.bfloat16)


def product(left, right, dims):
    return lax.dot_general(
        left, right, (dims, ((), ())), preferred_element_type=jnp.float32
    )


def rolled(values, shift, axis):
    return pltpu.roll(values, shift % values.shape[axis], axis)


def mix_kernel(weights_ref, spectrum_ref, out_ref):
    parts, channels, freqs = weights_ref.shape[:3]
    rows = weights_ref.shape[3]
    for freq in range(freqs):
        pieces = []
        for part in range(parts):
            total = weights_ref[part, 0, freq] * spectrum_ref[0, freq]
            for channel in range(1, channels):
                total = total + weights_ref[part, channel, freq] * spectrum_ref[channel, freq]
            pieces.append(total)
        out_ref[freq * rows : (freq + 1) * rows, :] = jnp.concatenate(pieces, axis=1)


def spread_kernel(scale, total_ref, spectrum_ref, out_ref):
    parts, channels, freqs, rows, cols = out_ref.shape
    for freq in range(freqs):
        for part in range(parts):
            piece = total_ref[freq * rows : (freq + 1) * rows, part * cols : (part + 1) * cols]
            for channel in range(channels):
                out_ref[part, channel, freq] = scale * piece * spectrum_ref[channel, freq]


def middle_kernel(
    modes_ref,
    basis_x_ref,
    lift_y_ref,
    drop_y_ref,
    blocks_ref,
    point_ref,
    before_ref,
    after_ref,
    edges_ref,
    flags_ref,
    grad_ref,
    out_ref,
    along_ref,
    field_ref,
    resid_ref,
    slope_ref,
    back_ref,
    drop_ref,
):
    parts, cells_x, cells_y, cells_z = point_ref.shape
    freqs, wide_x = basis_x_ref.shape
    rows = modes_ref.shape[0] // freqs
    tall = cells_y + rim
    group = 4
    lift_y = stacked_lanes(lift_y_ref[...], rows)
    drop_y = stacked_lanes(drop_y_ref[...], cells_y)
    block_high, block_low = halves(blocks_ref[...])

    def spread_x(pair, carry):
        first = pair * 2
        left = jnp.zeros((rows, modes_ref.shape[1]), jnp.float32)
        right = left
        for freq in range(freqs):
            value = modes_ref[freq * rows : (freq + 1) * rows, :]
            left = left + basis_x_ref[freq, first] * value
            right = right + basis_x_ref[freq, first + 1] * value
        along_ref[first] = left
        along_ref[first + 1] = right
        return carry

    lax.fori_loop(0, wide_x // 2, spread_x, 0)

    for start in range(0, wide_x, group):
        joined = jnp.concatenate([along_ref[start + k] for k in range(group)], axis=1)
        lifted = product(lift_y, stacked_rows(joined), ((1,), (0,)))
        width = modes_ref.shape[1]
        sheet = jnp.concatenate(
            [lifted[:, k * width : (k + 1) * width] for k in range(group)], axis=0
        )
        high, low = halves(sheet)
        full = product(high, block_high, ((1,), (0,)))
        full = full + product(low, block_high, ((1,), (0,)))
        full = full + product(high, block_low, ((1,), (0,)))
        for k in range(group):
            slab = start + k
            for part in range(parts):
                tile = full[k * tall : (k + 1) * tall, part * cells_z : (part + 1) * cells_z]
                if slab < halo:
                    inner = before_ref[part, slab]
                elif slab >= halo + cells_x:
                    inner = after_ref[part, slab - halo - cells_x]
                else:
                    inner = point_ref[part, slab - halo].astype(jnp.float32)
                field_ref[part, slab, :rim] = tile[:rim] + edges_ref[part, slab]
                field_ref[part, slab, rim:] = tile[rim:] + inner

    def beside(values):
        return (
            rolled(values, -1, 0),
            rolled(values, 1, 0),
            rolled(values, -1, 1),
            rolled(values, 1, 1),
        )

    def residuals(slab, carry):
        here = [field_ref[part, slab] for part in range(4)]
        slopes = []
        spreads = []
        for part in range(4):
            ahead = field_ref[part, slab + 1]
            behind = field_ref[part, slab - 1]
            up, down, right, left = beside(here[part])
            slopes.append(((ahead - behind) * 0.5, (up - down) * 0.5, (right - left) * 0.5))
            if part < 3:
                total = ((ahead + behind) + (up + down)) + (right + left)
                spreads.append(total - 6.0 * here[part])
        for i in range(3):
            value = here[0] * slopes[i][0] + here[1] * slopes[i][1] + here[2] * slopes[i][2]
            resid_ref[i, slab - 1] = value + slopes[3][i] - viscosity * spreads[i]
            for k in range(3):
                slope_ref[3 * k + i, slab - 1] = slopes[i][k][rim:]
        resid_ref[3, slab - 1] = slopes[0][0] + slopes[1][1] + slopes[2][2]
        return carry

    lax.fori_loop(1, wide_x - 1, residuals, 0)

    def adjoints(cell, carry):
        middle = cell + 1
        slab = cell + halo
        here = [resid_ref[i, middle] for i in range(3)]
        ahead = [resid_ref[i, middle + 1, rim:] for i in range(3)]
        behind = [resid_ref[i, middle - 1, rim:] for i in range(3)]
        core = [value[rim:] for value in here]
        drift_y = field_ref[1, slab]
        drift_z = field_ref[2, slab, rim:]
        drift_ahead = field_ref[0, slab + 1, rim:]
        drift_behind = field_ref[0, slab - 1, rim:]
        flag = flags_ref[cell]
        solid = flag > 0
        target = jnp.where(flag == 2, jnp.float32(inflow_speed), jnp.float32(0.0))
        source = resid_ref[3, middle]
        up, down = rolled(source, -1, 0)[rim:], rolled(source, 1, 0)[rim:]
        source_core = source[rim:]
        right, left = rolled(source_core, -1, 1), rolled(source_core, 1, 1)
        pull = [
            (resid_ref[3, middle + 1, rim:] - resid_ref[3, middle - 1, rim:]) * 0.5,
            (up - down) * 0.5,
            (right - left) * 0.5,
        ]
        press = []
        backs = []
        for k in range(3):
            up, down = rolled(here[k], -1, 0)[rim:], rolled(here[k], 1, 0)[rim:]
            right, left = rolled(core[k], -1, 1), rolled(core[k], 1, 1)
            press.append(((ahead[k] - behind[k]), (up - down), (right - left))[k] * 0.5)
            spread = ((ahead[k] + behind[k]) + (up + down)) + (right + left) - 6.0 * core[k]
            flux_y = drift_y * here[k]
            flux_z = drift_z * core[k]
            flux = drift_ahead * ahead[k] - drift_behind * behind[k]
            flux = flux + (rolled(flux_y, -1, 0)[rim:] - rolled(flux_y, 1, 0)[rim:])
            flux = flux + (rolled(flux_z, -1, 1) - rolled(flux_z, 1, 1))
            value = core[0] * slope_ref[3 * k, middle]
            value = value + core[1] * slope_ref[3 * k + 1, middle]
            value = value + core[2] * slope_ref[3 * k + 2, middle]
            value = value - pull[k] - 0.5 * flux - viscosity * spread
            velocity = field_ref[k, slab, rim:]
            offset = velocity - target if k == 0 else velocity
            value = value + penalty * jnp.where(solid, offset, jnp.float32(0.0))
            backs.append(value)
        backs.append(-((press[0] + press[1]) + press[2]))
        spot = pl.ds(pl.multiple_of(cell * cells_y, cells_y), cells_y)
        for part in range(4):
            grad_ref[part, cell] = backs[part].astype(grad_ref.dtype)
            back_ref[spot, part * cells_z : (part + 1) * cells_z] = backs[part]
        return carry

    lax.fori_loop(0, cells_x, adjoints, 0)

    high, low = halves(back_ref[...])
    flat = product(high, block_high, ((1,), (1,)))
    flat = flat + product(low, block_high, ((1,), (1,)))
    flat = flat + product(high, block_low, ((1,), (1,)))
    for start in range(0, cells_x, group):
        joined = jnp.concatenate(
            [flat[(start + k) * cells_y : (start + k + 1) * cells_y] for k in range(group)],
            axis=1,
        )
        dropped = product(drop_y, stacked_rows(joined), ((1,), (0,)))
        width = flat.shape[1]
        for k in range(group):
            drop_ref[start + k] = dropped[:, k * width : (k + 1) * width]

    def collect_x(pair, carry):
        first = pair * 2
        left = jnp.zeros((rows, modes_ref.shape[1]), jnp.float32)
        right = left
        for cell in range(cells_x):
            value = drop_ref[cell]
            left = left + basis_x_ref[first, cell + halo] * value
            right = right + basis_x_ref[first + 1, cell + halo] * value
        spot = pl.ds(pl.multiple_of(first * rows, rows), rows)
        out_ref[spot, :] = left
        spot = pl.ds(pl.multiple_of((first + 1) * rows, rows), rows)
        out_ref[spot, :] = right
        return carry

    lax.fori_loop(0, freqs // 2, collect_x, 0)


def middle(modes, basis_x, lift_y, drop_y, blocks, point, before, after, edges, flags):
    parts, cells_x, cells_y, cells_z = point.shape
    rows = drop_y.shape[0]
    lanes = modes.shape[1]
    wide_x = cells_x + 2 * halo
    tall = cells_y + rim
    vmem = pl.BlockSpec(memory_space=pltpu.VMEM)
    smem = pl.BlockSpec(memory_space=pltpu.SMEM)
    return pl.pallas_call(
        middle_kernel,
        name="middle",
        in_specs=[vmem, smem] + [vmem] * 8,
        out_specs=[vmem, vmem],
        out_shape=[
            jax.ShapeDtypeStruct(point.shape, jnp.bfloat16),
            jax.ShapeDtypeStruct(modes.shape, jnp.float32),
        ],
        scratch_shapes=[
            pltpu.VMEM((wide_x, rows, lanes), jnp.float32),
            pltpu.VMEM((parts, wide_x, tall, cells_z), jnp.float32),
            pltpu.VMEM((4, cells_x + 2, tall, cells_z), jnp.float32),
            pltpu.VMEM((9, cells_x + 2, cells_y, cells_z), jnp.float32),
            pltpu.VMEM((cells_x * cells_y, parts * cells_z), jnp.float32),
            pltpu.VMEM((cells_x, rows, lanes), jnp.float32),
        ],
    )(modes, basis_x, lift_y, drop_y, blocks, point, before, after, edges, flags)


def shift_pair(head, tail, axis):
    count = lax.axis_size(axis)
    before = lax.ppermute(tail, axis, [(i, (i + 1) % count) for i in range(count)])
    after = lax.ppermute(head, axis, [((i + 1) % count, i) for i in range(count)])
    return before, after


def exchange(chunks, axis):
    return lax.all_to_all(chunks, axis, 0, 0, tiled=True)


def reduce_scattered(chunks, axis):
    count = lax.axis_size(axis)
    pieces = exchange(chunks, axis)
    return jnp.sum(pieces.reshape((count, -1) + chunks.shape[1:]), 0)


def gathered(part, axis):
    count = lax.axis_size(axis)
    copies = jnp.broadcast_to(part[None], (count,) + part.shape)
    return exchange(copies.reshape((-1,) + part.shape[1:]), axis)


def body(spectrum, spec_weights, pointwise, mode_counts, flags):
    half_modes = spectrum.shape[3] // 2
    mode_span = 2 * half_modes
    local_freqs = spectrum.shape[1]
    parts, cells_x, cells_y, cells_z = pointwise.shape
    total_x = cells_x * lax.axis_size("gx")
    total_y = cells_y * lax.axis_size("gy")
    first_x = lax.axis_index("gx") * cells_x
    first_y = lax.axis_index("gy") * cells_y
    lanes = parts * mode_span
    vmem = pl.BlockSpec(memory_space=pltpu.VMEM)

    with jax.named_scope("mix"):
        chunks = pl.pallas_call(
            mix_kernel,
            name="mix",
            in_specs=[vmem, vmem],
            out_specs=vmem,
            out_shape=jax.ShapeDtypeStruct((local_freqs * mode_span, lanes), jnp.float32),
        )(spec_weights, spectrum)
    with jax.named_scope("sum_modes"):
        part = reduce_scattered(chunks, "gx")

    with jax.named_scope("halo_x"):
        head = pointwise[:, :halo].astype(jnp.float32)
        tail = pointwise[:, cells_x - halo :].astype(jnp.float32)
        before, after = shift_pair(head, tail, "gx")
    with jax.named_scope("halo_y"):
        sides = []
        for low in (0, cells_y - halo):
            own = pointwise[:, :, low : low + halo].astype(jnp.float32)
            ends = [before[:, :, low : low + halo], after[:, :, low : low + halo]]
            sides.append(jnp.concatenate([ends[0], own, ends[1]], 1))
        under, over = shift_pair(sides[0], sides[1], "gy")
        gap = jnp.zeros((parts, cells_x + 2 * halo, rim - 2 * halo, cells_z), jnp.float32)
        edges = jnp.concatenate([over, gap, under], 2)

    places_x = first_x - halo + jnp.arange(cells_x + 2 * halo, dtype=jnp.int32)
    rows_y = jnp.arange(cells_y + rim, dtype=jnp.int32)
    places_y = first_y + jnp.where(rows_y < halo, cells_y + rows_y, rows_y - rim)
    basis_x = mode_basis(mode_counts[0], total_x, places_x, half_modes)
    basis_y = mode_basis(mode_counts[1], total_y, places_y, half_modes)
    basis_z = mode_basis(
        mode_counts[2], cells_z, jnp.arange(cells_z, dtype=jnp.int32), half_modes
    )
    lift_y = jnp.tile(basis_y.T, (1, 3))
    drop_y = jnp.tile(basis_y[:, rim:], (1, 3))
    same = jnp.arange(lanes)[:, None] // mode_span == jnp.arange(parts * cells_z)[None] // cells_z
    blocks = jnp.where(same, jnp.tile(basis_z, (parts, parts)), jnp.float32(0.0))
    columns = jnp.broadcast_to(flags[:, :, None], flags.shape + (cells_z,))

    with jax.named_scope("share_modes"):
        modes = gathered(part, "gx")
    with jax.named_scope("share_freqs"):
        modes = gathered(modes, "gy")
    with jax.named_scope("middle"):
        grad_field, projected = middle(
            modes, basis_x, lift_y, drop_y, blocks, pointwise, before, after, edges, columns
        )
    with jax.named_scope("sum_y"):
        summed = reduce_scattered(projected, "gy")
    with jax.named_scope("sum_x"):
        summed = reduce_scattered(summed, "gx")
    with jax.named_scope("share_sums"):
        total = gathered(summed, "gx")
    scale = mode_span**1.5 / math.sqrt(total_x * total_y * cells_z)
    with jax.named_scope("spread"):
        grad_weights = pl.pallas_call(
            functools.partial(spread_kernel, scale),
            name="spread",
            in_specs=[vmem, vmem],
            out_specs=vmem,
            out_shape=jax.ShapeDtypeStruct(spec_weights.shape, jnp.float32),
        )(total, spectrum)
    return (grad_field, grad_weights)


def solution(mesh):
    return jax.shard_map(
        body,
        mesh=mesh,
        in_specs=(
            P("gx", "gy", None, None),
            P(None, "gx", "gy", None, None),
            P(None, "gx", "gy", None),
            P(),
            P("gx", "gy"),
        ),
        out_specs=(P(None, "gx", "gy", None), P(None, "gx", "gy", None, None)),
        check_vma=False,
    )
```

time: 149 us -> 140 us (0.940)
  waiting for transfers between devices: 33.7 us -> 13 us
  blocking collectives: 33.8 us -> 47.9 us
  Pallas kernels: 0 us -> 12.5 us
  other arithmetic: 13.6 us -> 4.99 us
  matrix products: 6.77 us -> 0 us
  starting transfers between devices: 47.1 us -> 52.7 us
  local copies, waits for them, and re-layouts: 10.5 us -> 5.66 us
    all_to_all x4 -> x3, waiting for transfers between devices: 33.7 us -> 7.41 us  [exchange(): return lax.all_to_all(chunks, axis, 0, 0, tiled=True)]
    all_to_all x2 -> x3, blocking collectives: 33.8 us -> 47.9 us  [exchange(): return lax.all_to_all(chunks, axis, 0, 0, tiled=True)]
    pallas_call x0 -> x3, Pallas kernels: none -> 12.5 us  [the longest x1 9.28 us: middle(): pl.pallas_call(middle_kernel, name='middle', in_specs=[vmem, smem] + [vme...]
    all_to_all x4 -> x3, starting transfers between devices: 26.5 us -> 38.3 us  [exchange(): return lax.all_to_all(chunks, axis, 0, 0, tiled=True)]
    ppermute x2, starting transfers between devices: 15 us -> 7.35 us  [shift_pair(): lax.ppermute(head, axis, [((i + 1) % count, i) for i in range(count)])]
    dot_general x6 -> x0, matrix products: 6.77 us -> none  [the longest x1 2.61 us: body(): section = jnp.einsum('porq,px->oxrq', modes, basis_x, precision=high)]
    ppermute x2, waiting for transfers between devices: 0.01 us -> 5.63 us  [shift_pair(): lax.ppermute(head, axis, [((i + 1) % count, i) for i in range(count)])]
    slice x9 -> x3, local copies, waits for them, and re-layouts: 2.8 us -> 0.66 us  [the longest x1 0.65 us: body(): mode_counts[2]]
  transfers between devices with their start and end apart: 8 -> 7, of which waited for: 4 -> 3; matrix products, arithmetic and copies ran while one was open for 11% -> 6% of each run, Pallas kernels for 0% -> 0%
where the time goes in v2:
time: 140 us; the launch traced here: 138 us
  starting transfers between devices  52.7 us (38%)
  blocking collectives  47.9 us (34%)
  waiting for transfers between devices  13 us (9%)
  Pallas kernels  12.5 us (9%)
  local copies, waits for them, and re-layouts  5.66 us (4%)
  other arithmetic  4.99 us (4%)
    all_to_all x3, blocking collectives, exchange(): return lax.all_to_all(chunks, axis, 0, 0, tiled=True)  47.9 us
    all_to_all x3, starting transfers between devices, exchange(): return lax.all_to_all(chunks, axis, 0, 0, tiled=True)  38.3 us
    pallas_call x1, Pallas kernels, middle(): pl.pallas_call(middle_kernel, name='middle', in_specs=[vmem, smem] + [vme...  9.28 us
    all_to_all x3, waiting for transfers between devices, exchange(): return lax.all_to_all(chunks, axis, 0, 0, tiled=True)  7.41 us
    ppermute x2, starting transfers between devices, shift_pair(): lax.ppermute(head, axis, [((i + 1) % count, i) for i in range(count)])  7.35 us
    ppermute x2, starting transfers between devices, shift_pair(): lax.ppermute(tail, axis, [(i, (i + 1) % count) for i in range(count)])  6.99 us
    ppermute x2, waiting for transfers between devices, shift_pair(): lax.ppermute(head, axis, [((i + 1) % count, i) for i in range(count)])  5.63 us
  transfers between devices with their start and end apart: 7, of which 3 were waited for; matrix products, arithmetic and copies ran while one was open for 6% of the time, Pallas kernels for 0%

profile of v2, /device:TPU:1, one launch (start us, length us, event | category | flops | bytes accessed | tf_op | source)
XLA Modules:
  0.0 137.7 jit_solution(2286744129482360522)
XLA Ops:
  0.6 1.7 %mix.1 = f32[64,128]{1,0:T(8,128)} custom-call(f32[4,1,2,32,32]{4,3,2,1,0:T(8,128)} %weights_ref.1, f32[1,2,32,32]{3,2,1,0:T(8,128)} %spectrum_ref.3), custom_call_target="tpu_custom_call" | custom-call | tf_op jit(solution)/shard_map/mix/mix/pallas_call | solution.py:324
  2.3 17.0 %all-to-all-start = ((f32[32,2,128]{2,1,0:T(2,128)}), f32[32,2,128]{2,1,0:T(2,128)S(1)}, u32[]{:S(2)}, u32[]{:S(2)}) async-start(f32[32,2,128]{2,1,0:T(2,128)} %bitcast.19), calls=%async_computation | async-start | bytes 65536 | tf_op jit(solution)/shard_map/sum_modes/all_to_all | solution.py:296
  19.4 5.3 %collective-permute-start.1 = (f32[4,2,16,128]{3,2,1,0:T(8,128)S(1)}, f32[4,2,16,128]{3,2,1,0:T(8,128)S(1)}, u32[]{:S(2)}, u32[]{:S(2)}) collective-permute-start(f32[4,2,16,128]{3,2,1,0:T(8,128)S(1)} %get-tuple-element.8), channel_id=1, source_target_pairs={{16,0},{32,16},{48,32},{64,48},{80,64},{96,80},{112,96},{128,112},... | collective-permute-start | bytes 196616 | tf_op jit(solution)/shard_map/halo_x/ppermute | solution.py:291
  24.7 1.9 %collective-permute-start = (f32[4,2,16,128]{3,2,1,0:T(8,128)S(1)}, f32[4,2,16,128]{3,2,1,0:T(8,128)S(1)}, u32[]{:S(2)}, u32[]{:S(2)}) collective-permute-start(f32[4,2,16,128]{3,2,1,0:T(8,128)S(1)} %get-tuple-element.9), channel_id=1, source_target_pairs={{0,16},{16,32},{32,48},{48,64},{64,80},{80,96},{96,112},{112,128},... | collective-permute-start | bytes 196616 | tf_op jit(solution)/shard_map/halo_x/ppermute | solution.py:290
  26.8 0.6 copy-done.5
  27.4 0.6 fusion.20
  28.1 0.7 broadcast_compare_fusion
  28.7 0.6 broadcast_compare_fusion.1
  29.3 0.6 iota_compare_fusion
  30.1 0.1 select_multiply_fusion
  30.2 0.8 select_multiply_fusion.1.basis_x_ref
  31.0 0.8 bitcast_select_fusion.blocks_ref
  32.0 0.6 broadcast_in_dim.113
  32.6 11.4 %all-to-all-start.1 = ((f32[32,2,128]{2,1,0:T(2,128)}), f32[32,2,128]{2,1,0:T(2,128)S(1)}, u32[]{:S(2)}, u32[]{:S(2)}) async-start(f32[32,2,128]{2,1,0:T(2,128)} %broadcast_in_dim.113), calls=%async_computation.1 | async-start | bytes 65536 | tf_op jit(solution)/shard_map/share_modes/all_to_all | solution.py:296
  44.1 0.5 copy-done.3
  44.7 5.1 %collective-permute-start.3 = (f32[4,20,2,128]{3,2,1,0:T(2,128)S(1)}, f32[4,20,2,128]{3,2,1,0:T(2,128)S(1)}, u32[]{:S(2)}, u32[]{:S(2)}) collective-permute-start(f32[4,20,2,128]{3,2,1,0:T(2,128)S(1)} %pad_maximum_fusion.2), channel_id=1, source_target_pairs={{0,1},{1,2},{2,3},{3,4},{4,5},{5,6},{6,7},{7,8},{8,9},{9,10},{10,1... | collective-permute-start | bytes 245768 | tf_op jit(solution)/shard_map/halo_y/ppermute | solution.py:290
  49.7 6.5 %all-to-all-done.1 = f32[32,2,128]{2,1,0:T(2,128)S(1)} async-done(((f32[32,2,128]{2,1,0:T(2,128)}), f32[32,2,128]{2,1,0:T(2,128)S(1)}, u32[]{:S(2)}, u32[]{:S(2)}) %all-to-all-start.1) | async-done | bytes 32800 | tf_op jit(solution)/shard_map/share_modes/all_to_all | solution.py:296
  56.3 0.8 broadcast_in_dim.115
  57.1 9.9 %all-to-all-start.2 = ((f32[16,64,128]{2,1,0:T(8,128)}), f32[16,64,128]{2,1,0:T(8,128)S(1)}, u32[]{:S(2)}, u32[]{:S(2)}) async-start(f32[16,64,128]{2,1,0:T(8,128)} %broadcast_in_dim.115), calls=%async_computation.2 | async-start | bytes 1048576 | tf_op jit(solution)/shard_map/share_freqs/all_to_all | solution.py:296
  67.0 2.0 %collective-permute-start.2 = (f32[4,20,2,128]{3,2,1,0:T(2,128)S(1)}, f32[4,20,2,128]{3,2,1,0:T(2,128)S(1)}, u32[]{:S(2)}, u32[]{:S(2)}) collective-permute-start(f32[4,20,2,128]{3,2,1,0:T(2,128)S(1)} %pad_maximum_fusion.1), channel_id=1, source_target_pairs={{1,0},{2,1},{3,2},{4,3},{5,4},{6,5},{7,6},{8,7},{9,8},{10,9},{11,1... | collective-permute-start | bytes 245768 | tf_op jit(solution)/shard_map/halo_y/ppermute | solution.py:291
  69.1 0.1 select_multiply_fusion.2
  69.2 0.7 copy.9.drop_y_ref
  69.9 0.7 tile.13.lift_y_ref
  70.7 5.6 %collective-permute-done.2 = f32[4,20,2,128]{3,2,1,0:T(2,128)S(1)} collective-permute-done((f32[4,20,2,128]{3,2,1,0:T(2,128)S(1)}, f32[4,20,2,128]{3,2,1,0:T(2,128)S(1)}, u32[]{:S(2)}, u32[]{:S(2)}) %collective-permute-start.2) | collective-permute-done | bytes 81952 | tf_op jit(solution)/shard_map/halo_y/ppermute | solution.py:291
  76.3 0.8 pad_maximum_fusion.edges_ref
  77.1 0.9 all-to-all-done.2
  78.0 0.8 broadcast_in_dim.130.flags_ref
  78.8 9.3 %middle.1 = (bf16[4,16,16,128]{3,2,1,0:T(8,128)(2,1)}, f32[1024,128]{1,0:T(8,128)}) custom-call(f32[1024,128]{1,0:T(8,128)} %bitcast.14, f32[32,20]{1,0:T(8,128)} %select_multiply_fusion.1.basis_x_ref, f32[24,96]{1,0:T(8,128)} %tile.13.lift_y_ref, f32[32,48]{1,0:T(8,128)} %copy.9.drop_y_ref, f32[128,512]{1,0:T(8,128)} %bitcast_select_fusion.blocks_ref, ...), custom_call_target="tpu_custom_call" | custom-call | tf_op jit(solution)/shard_map/middle/middle/pallas_call | solution.py:268
  88.1 16.9 %all_to_all.49 = f32[16,64,128]{2,1,0:T(8,128)S(1)} all-to-all(f32[16,64,128]{2,1,0:T(8,128)} %bitcast.16), channel_id=1, replica_groups=mesh['gx'=32,'gy'=16] {'gy'}, dimensions={0} | all-to-all | bytes 1048576 | tf_op jit(solution)/shard_map/sum_y/all_to_all | solution.py:296
  105.1 15.2 %all_to_all.50 = f32[32,2,128]{2,1,0:T(2,128)S(1)} all-to-all(f32[32,2,128]{2,1,0:T(2,128)S(1)} %bitcast.18), channel_id=1, replica_groups=mesh['gx'=32,'gy'=16] {'gx'}, dimensions={0} | all-to-all | bytes 65536 | tf_op jit(solution)/shard_map/sum_x/all_to_all | solution.py:296
  120.3 15.8 %all_to_all.51 = f32[32,2,128]{2,1,0:T(2,128)} all-to-all(f32[32,2,128]{2,1,0:T(2,128)S(1)} %broadcast_in_dim.131), channel_id=1, replica_groups=mesh['gx'=32,'gy'=16] {'gx'}, dimensions={0} | all-to-all | bytes 65536 | tf_op jit(solution)/shard_map/share_sums/all_to_all | solution.py:296
  136.1 1.6 %spread.1 = f32[4,1,2,32,32]{4,3,2,1,0:T(8,128)} custom-call(f32[64,128]{1,0:T(8,128)} %bitcast.20, f32[1,2,32,32]{3,2,1,0:T(8,128)} %spectrum_ref.3), custom_call_target="tpu_custom_call" | custom-call | tf_op jit(solution)/shard_map/spread/spread/pallas_call | solution.py:378
  (36 shorter events, 0.6 us)
Async XLA Ops:
  0.6 18.7 %copy-start.1 = (bf16[4,16,16,128]{3,2,1,0:T(8,128)(2,1)S(1)}, bf16[4,16,16,128]{3,2,1,0:T(8,128)(2,1)}, u32[]{:S(2)}) copy-start(bf16[4,16,16,128]{3,2,1,0:T(8,128)(2,1)} %point_ref.1) | copy-start | bytes 786436
  2.3 29.6 %all-to-all-start = ((f32[32,2,128]{2,1,0:T(2,128)}), f32[32,2,128]{2,1,0:T(2,128)S(1)}, u32[]{:S(2)}, u32[]{:S(2)}) async-start(f32[32,2,128]{2,1,0:T(2,128)} %bitcast.19), calls=%async_computation | async-start | bytes 65536 | tf_op jit(solution)/shard_map/sum_modes/all_to_all | solution.py:296
  19.4 12.5 %collective-permute-start.1 = (f32[4,2,16,128]{3,2,1,0:T(8,128)S(1)}, f32[4,2,16,128]{3,2,1,0:T(8,128)S(1)}, u32[]{:S(2)}, u32[]{:S(2)}) collective-permute-start(f32[4,2,16,128]{3,2,1,0:T(8,128)S(1)} %get-tuple-element.8), channel_id=1, source_target_pairs={{16,0},{32,16},{48,32},{64,48},{80,64},{96,80},{112,96},{128,112},... | collective-permute-start | bytes 196616 | tf_op jit(solution)/shard_map/halo_x/ppermute | solution.py:291
  24.7 19.3 %collective-permute-start = (f32[4,2,16,128]{3,2,1,0:T(8,128)S(1)}, f32[4,2,16,128]{3,2,1,0:T(8,128)S(1)}, u32[]{:S(2)}, u32[]{:S(2)}) collective-permute-start(f32[4,2,16,128]{3,2,1,0:T(8,128)S(1)} %get-tuple-element.9), channel_id=1, source_target_pairs={{0,16},{16,32},{32,48},{48,64},{64,80},{80,96},{96,112},{112,128},... | collective-permute-start | bytes 196616 | tf_op jit(solution)/shard_map/halo_x/ppermute | solution.py:290
  26.8 0.7 copy-start.5
  31.9 0.7 copy-start.2
  32.6 23.7 %all-to-all-start.1 = ((f32[32,2,128]{2,1,0:T(2,128)}), f32[32,2,128]{2,1,0:T(2,128)S(1)}, u32[]{:S(2)}, u32[]{:S(2)}) async-start(f32[32,2,128]{2,1,0:T(2,128)} %broadcast_in_dim.113), calls=%async_computation.1 | async-start | bytes 65536 | tf_op jit(solution)/shard_map/share_modes/all_to_all | solution.py:296
  44.0 0.6 copy-start.3
  44.7 26.0 %collective-permute-start.3 = (f32[4,20,2,128]{3,2,1,0:T(2,128)S(1)}, f32[4,20,2,128]{3,2,1,0:T(2,128)S(1)}, u32[]{:S(2)}, u32[]{:S(2)}) collective-permute-start(f32[4,20,2,128]{3,2,1,0:T(2,128)S(1)} %pad_maximum_fusion.2), channel_id=1, source_target_pairs={{0,1},{1,2},{2,3},{3,4},{4,5},{5,6},{6,7},{7,8},{8,9},{9,10},{10,1... | collective-permute-start | bytes 245768 | tf_op jit(solution)/shard_map/halo_y/ppermute | solution.py:290
  57.1 20.9 %all-to-all-start.2 = ((f32[16,64,128]{2,1,0:T(8,128)}), f32[16,64,128]{2,1,0:T(8,128)S(1)}, u32[]{:S(2)}, u32[]{:S(2)}) async-start(f32[16,64,128]{2,1,0:T(8,128)} %broadcast_in_dim.115), calls=%async_computation.2 | async-start | bytes 1048576 | tf_op jit(solution)/shard_map/share_freqs/all_to_all | solution.py:296
  67.0 9.3 %collective-permute-start.2 = (f32[4,20,2,128]{3,2,1,0:T(2,128)S(1)}, f32[4,20,2,128]{3,2,1,0:T(2,128)S(1)}, u32[]{:S(2)}, u32[]{:S(2)}) collective-permute-start(f32[4,20,2,128]{3,2,1,0:T(2,128)S(1)} %pad_maximum_fusion.1), channel_id=1, source_target_pairs={{1,0},{2,1},{3,2},{4,3},{5,4},{6,5},{7,6},{8,7},{9,8},{10,9},{11,1... | collective-permute-start | bytes 245768 | tf_op jit(solution)/shard_map/halo_y/ppermute | solution.py:291
  70.7 7.3 %copy-start.4 = (s32[16,16]{1,0:T(8,128)S(1)}, s32[16,16]{1,0:T(8,128)}, u32[]{:S(2)}) copy-start(s32[16,16]{1,0:T(8,128)} %param.9) | copy-start | bytes 3076
  78.0 0.8 copy-start
